TPU v7x, 32 devices: a whole 2x2x4 slice. The times are simulated.
32 devices in a mesh: groups: 2 (over x), seq: 16 (over z, y, core).
Axes of the slice: x: 2, y: 2, z: 4, core: 2. Of those that a mesh axis runs over, the one named last changes fastest.
Arguments:
- queries: bfloat16 [4096, 8192], P(('groups', 'seq')), parts along dimension 0, may hold values from -4.5 to 4.5
- keyvalue: bfloat16 [4096, 2048], P(('groups', 'seq')), parts along dimension 0, may hold values from -4.5 to 4.5
- doc_ids: int32 [4096], P(('groups', 'seq')), parts along dimension 0, may hold values from 0 to 7, never falling along the last dimension, each value on 1 to 512 neighbouring positions
- owner_tiles: int32 [32, 2], P(('groups', 'seq')), parts along dimension 0, may hold values from 0 to 15, as said below
- tile_counts: int32 [32], P(('groups', 'seq')), parts along dimension 0, may hold values from 0 to 2, as said below
Outputs:
- owned: bfloat16 [8192, 8192], P(('groups', 'seq')), parts along dimension 0
There are 2 independent parts, one for each index of `groups`. A program takes and returns all parts, laid end to end along the dimension named above; each array names one. Nothing has to cross between parts.
Inputs may be any that keep to these rules, and one draw needn't show every extreme that they name: `owner_tiles`: over the slots below each owner's count, every tile 0 to 15 is listed exactly once; the other slots hold 0. Tile t is listed either by its holder, the owner o with o * 128 <= t * 128 < (o + 1) * 128, or by the holder's partner, the owner whose index differs from the holder's by half the number of owners. `tile_counts`: the counts sum to 16; each is 0, 1 or 2, some owner has 2, and an owner has 2 exactly when its partner has 0.
All inputs are finite; a program needn't handle non-finite values.
Results may differ from a plain program's by a relative error of at most 0.0034.
Values may be sent and summed in bfloat16 or wider, within the bound.
A program may use at most 64 MiB of HBM per device.

v0:
```python
import jax
import jax.numpy as jnp
from jax import lax
from jax.sharding import PartitionSpec as P

QUERY_HEADS = 64
KEY_VALUE_HEADS = 8
HEAD_WIDTH = 128
TILE = 128
DOCUMENT_LIMIT = 512


def from_behind(shard, axis, by):
    count = lax.axis_size(axis)
    pairs = [(i, i + by) for i in range(count) if 0 <= i + by < count]
    return lax.ppermute(shard, axis, pairs)


def attend(queries, keys, value_rows, allowed):
    scale = queries.shape[-1] ** (-0.5)
    scores = jnp.einsum("rhgd,khd->hgrk", queries, keys, preferred_element_type=jnp.float32) * scale
    scores = jnp.where(allowed[None, None], scores, -jnp.inf)
    row_top = jnp.max(scores, axis=3, keepdims=True)
    exponent = jnp.exp(scores - row_top)
    totals = jnp.sum(exponent, axis=3, keepdims=True)
    weights = exponent.astype(jnp.bfloat16)
    mixed_rows = jnp.einsum(
        "hgrk,khd->rhgd", weights, value_rows, preferred_element_type=jnp.float32
    )
    return (mixed_rows / jnp.transpose(totals, (2, 0, 1, 3))).astype(jnp.bfloat16)


def deliver_owners(head_rows, all_lists, owner_tiles, seq_count, width):
    slots_dev = owner_tiles.shape[1]
    slot_rows = slots_dev * TILE
    tile_rows = jnp.arange(TILE, dtype=jnp.int32)
    row_index = jnp.transpose(all_lists)[:, None, :] * TILE + tile_rows[None, :, None]
    send_rows = jnp.take(head_rows, row_index.reshape(slot_rows, seq_count), axis=0)
    received = lax.all_to_all(send_rows, "seq", split_axis=1, concat_axis=1, tiled=True)
    return received.reshape(slot_rows, width)


def local(queries, keyvalue, doc_ids, owner_tiles, tile_counts):
    seq_count = lax.axis_size("seq")
    token_per_holder = queries.shape[0]
    width = queries.shape[1]
    head_share = QUERY_HEADS // seq_count
    group_width = QUERY_HEADS // KEY_VALUE_HEADS
    head_cols = head_share * HEAD_WIDTH
    slots_dev = owner_tiles.shape[1]
    reach_devs = (DOCUMENT_LIMIT - 1) // token_per_holder + 1
    doc_marks = doc_ids + 1
    kv_parts = [keyvalue]
    mark_parts = [doc_marks]
    for shift_by in range(1, reach_devs + 1):
        far_kv, far_marks = from_behind((keyvalue, doc_marks), "seq", shift_by)
        kv_parts.insert(0, far_kv)
        mark_parts.insert(0, far_marks)
    kv_near = jnp.concatenate(kv_parts, axis=0)
    near_marks = jnp.concatenate(mark_parts, axis=0)
    near_rows = kv_near.shape[0]
    keyvalue_grouped = kv_near.reshape(near_rows, KEY_VALUE_HEADS, 2, HEAD_WIDTH)
    q_place = jnp.arange(token_per_holder, dtype=jnp.int32) + reach_devs * token_per_holder
    k_place = jnp.arange(near_rows, dtype=jnp.int32)
    allowed = (doc_marks[:, None] == near_marks[None, :]) & (k_place[None, :] <= q_place[:, None])
    local_out = attend(
        queries.reshape(token_per_holder, KEY_VALUE_HEADS, group_width, HEAD_WIDTH),
        keyvalue_grouped[:, :, 0],
        keyvalue_grouped[:, :, 1],
        allowed,
    )
    local_out = local_out.reshape(token_per_holder, width)
    all_lists = lax.all_gather(owner_tiles, "seq", axis=0, tiled=True)
    out_send = local_out.reshape(token_per_holder, seq_count, head_cols)
    head_rows = lax.all_to_all(out_send, "seq", split_axis=1, concat_axis=0, tiled=True).reshape(
        token_per_holder * seq_count, head_cols
    )
    owned = deliver_owners(head_rows, all_lists, owner_tiles, seq_count, width)
    live = jnp.repeat(jnp.arange(slots_dev, dtype=jnp.int32) < tile_counts[0], TILE)
    return jnp.where(live[:, None], owned, jnp.zeros((), jnp.bfloat16))


def solution(mesh):
    placed = (
        P(("groups", "seq"), None),
        P(("groups", "seq"), None),
        P(("groups", "seq")),
        P(("groups", "seq"), None),
        P(("groups", "seq")),
    )
    return jax.shard_map(
        local, mesh=mesh, in_specs=placed, out_specs=P(("groups", "seq"), None), check_vma=False
    )
```

profile of v0, /device:TPU:15, one launch (start us, length us, event | category | flops | bytes accessed | tf_op | source)
XLA Modules:
  0.0 285.1 jit_solution(12777522837619255446)
XLA Ops:
  0.0 0.7 broadcast_add_fusion
  0.7 3.2 %collective-permute-start.4 = (s32[128]{0:T(128)S(1)}, s32[128]{0:T(128)S(1)}, u32[]{:S(2)}, u32[]{:S(2)}) collective-permute-start(s32[128]{0:T(128)S(1)} %broadcast_add_fusion), channel_id=1, source_target_pairs={{0,4},{1,5},{2,6},{3,7},{4,8},{5,9},{6,10},{7,11},{8,12},{9,13},{1... | collective-permute-start | bytes 1544 | tf_op jit(solution)/shard_map/ppermute | solution.py:16
  3.9 4.0 %collective-permute-start.5 = (s32[128]{0:T(128)S(1)}, s32[128]{0:T(128)S(1)}, u32[]{:S(2)}, u32[]{:S(2)}) collective-permute-start(s32[128]{0:T(128)S(1)} %broadcast_add_fusion), channel_id=1, source_target_pairs={{0,3},{1,4},{2,5},{3,6},{4,7},{5,8},{6,9},{7,10},{8,11},{9,12},{10... | collective-permute-start | bytes 1544 | tf_op jit(solution)/shard_map/ppermute | solution.py:16
  8.0 1.9 collective-permute-start.6
  9.9 3.4 %collective-permute-start.7 = (s32[128]{0:T(128)S(1)}, s32[128]{0:T(128)S(1)}, u32[]{:S(2)}, u32[]{:S(2)}) collective-permute-start(s32[128]{0:T(128)S(1)} %broadcast_add_fusion), channel_id=1, source_target_pairs={{0,1},{1,2},{2,3},{3,4},{4,5},{5,6},{6,7},{7,8},{8,9},{9,10},{10,1... | collective-permute-start | bytes 1544 | tf_op jit(solution)/shard_map/ppermute | solution.py:16
  13.3 1.3 copy.52
  14.6 1.9 collective-permute-start
  16.6 2.2 copy.71
  18.8 1.9 collective-permute-start.1
  20.7 1.9 collective-permute-start.2
  22.7 2.2 collective-permute-start.3
  24.9 0.2 fusion.11
  25.1 5.3 %collective-permute-done = bf16[128,2048]{0,1:T(8,128)(2,1)S(1)} collective-permute-done((bf16[128,2048]{0,1:T(8,128)(2,1)S(1)}, bf16[128,2048]{0,1:T(8,128)(2,1)S(1)}, u32[]{:S(2)}, u32[]{:S(2)}) %collective-permute-start) | collective-permute-done | bytes 524320 | tf_op jit(solution)/shard_map/ppermute | solution.py:16
  30.5 9.0 %collective-permute-done.1 = bf16[128,2048]{0,1:T(8,128)(2,1)S(1)} collective-permute-done((bf16[128,2048]{0,1:T(8,128)(2,1)S(1)}, bf16[128,2048]{0,1:T(8,128)(2,1)S(1)}, u32[]{:S(2)}, u32[]{:S(2)}) %collective-permute-start.1) | collective-permute-done | bytes 524320 | tf_op jit(solution)/shard_map/ppermute | solution.py:16
  39.6 10.8 %collective-permute-done.2 = bf16[128,2048]{0,1:T(8,128)(2,1)S(1)} collective-permute-done((bf16[128,2048]{0,1:T(8,128)(2,1)S(1)}, bf16[128,2048]{0,1:T(8,128)(2,1)S(1)}, u32[]{:S(2)}, u32[]{:S(2)}) %collective-permute-start.2) | collective-permute-done | bytes 524320 | tf_op jit(solution)/shard_map/ppermute | solution.py:16
  50.6 5.5 %collective-permute-done.3 = bf16[128,2048]{0,1:T(8,128)(2,1)S(1)} collective-permute-done((bf16[128,2048]{0,1:T(8,128)(2,1)S(1)}, bf16[128,2048]{0,1:T(8,128)(2,1)S(1)}, u32[]{:S(2)}, u32[]{:S(2)}) %collective-permute-start.3) | collective-permute-done | bytes 524320 | tf_op jit(solution)/shard_map/ppermute | solution.py:16
  56.2 0.1 constant_dynamic-update-slice_fusion
  56.4 1.5 copy-done.1
  57.8 5.9 %fusion.2 = (f32[8,8,128]{2,1,0:T(8,128)S(1)}, f32[8,640,128,8]{2,1,3,0:T(8,128)S(1)}) fusion(pred[128,640]{0,1:T(8,128)(4,1)S(1)} %fusion.11, bf16[128,8,8,128]{3,2,1,0:T(8,128)(2,1)S(1)} %bitcast.69, bf16[640,8,2,128]{0,3,2,1:T(8,128)(2,1)} %bitcast.71), kind=kOutput, calls=%fused_computation.5 | convolution fusion | flops 1357897728 | bytes 24494080 | tf_op jit(solution)/shard_map/rhgd,khd->hgrk/dot_general | solution.py:21
  63.8 5.7 %fusion = f32[8,8,128]{2,1,0:T(8,128)} fusion(f32[8,640,128,8]{2,1,3,0:T(8,128)S(1)} %get-tuple-element.6, f32[8,8,128]{2,1,0:T(8,128)S(1)} %get-tuple-element.5, pred[128,640]{0,1:T(8,128)(4,1)S(1)} %fusion.11), kind=kLoop, calls=%fused_computation.3 | loop fusion | flops 20963328 | bytes 21118976 | tf_op jit(solution)/shard_map/reduce_sum | solution.py:25
  69.5 7.8 %fusion.6 = bf16[128,8,8,128]{0,3,2,1:T(8,128)(2,1)} fusion(f32[8,640,128,8]{2,1,3,0:T(8,128)S(1)} %get-tuple-element.6, f32[8,8,128]{2,1,0:T(8,128)S(1)} %get-tuple-element.5, pred[128,640]{0,1:T(8,128)(4,1)} %copy-done.2, f32[128,8,8]{0,2,1:T(8,128)} %bitcast.76, bf16[640,8,2,128]{0,3,2,1:T(8,128)(2,1)} %bitcast.72), kind=kOutput, calls=%fused_computation.10 | convolution fusion | flops 1365245952 | bytes 24526848 | tf_op jit(solution)/shard_map/hgrk,khd->rhgd/dot_general | solution.py:27
  77.2 6.8 %all-to-all-start = ((bf16[128,16,512]{0,2,1:T(8,128)(2,1)}), bf16[128,16,512]{0,2,1:T(8,128)(2,1)S(1)}, u32[]{:S(2)}, u32[]{:S(2)}) async-start(bf16[128,16,512]{0,2,1:T(8,128)(2,1)} %bitcast.74), calls=%async_computation | async-start | bytes 4194304 | tf_op jit(solution)/shard_map/all_to_all | solution.py:75
  84.1 56.9 %all-gather = s32[16,1,2]{2,1,0:T(1,128)S(1)} all-gather(s32[1,1,2]{2,1,0:T(1,128)S(1)} %bitcast.77), channel_id=1, replica_groups=mesh['groups'=2,'seq'=16] {'seq'}, dimensions={0}, use_global_device_ids=true | all-gather | bytes 136 | tf_op jit(solution)/shard_map/all_gather | solution.py:73
  141.4 1.3 copy-done
  142.7 2.9 %copy.61 = bf16[16,128,1,512]{3,1,0,2:T(8,128)(2,1)S(1)} copy(bf16[16,128,1,512]{1,3,0,2:T(8,128)(2,1)} %bitcast.70) | data formatting | bytes 4194304 | tf_op jit(solution)/shard_map/all_to_all | solution.py:75
  145.5 17.3 %gather_fusion = bf16[4096,512]{1,0:T(8,128)(2,1)} fusion(bf16[2048,512]{1,0:T(8,128)(2,1)S(1)} %bitcast.67, s32[4096]{0:T(1024)S(1)} %broadcast_clamp_fusion), kind=kCustom, calls=%fused_computation | custom fusion | bytes 8404992 | tf_op jit(solution)/shard_map/jit(_take)/gather | solution.py:38
  162.9 7.5 %copy_select_fusion = bf16[256,16,512]{2,0,1:T(8,128)(2,1)} fusion(bf16[256,16,512]{2,1,0:T(8,128)(2,1)} %bitcast.68, pred[256,16]{0,1:T(8,128)(4,1)S(1)} %compare_and_fusion), kind=kLoop, calls=%fused_computation.11 | loop fusion | flops 2097152 | bytes 8392704 | tf_op jit(solution)/shard_map/jit(_take)/select_n | solution.py:38
  170.4 4.9 %all-to-all-start.1 = ((bf16[256,16,512]{2,0,1:T(8,128)(2,1)}), bf16[256,16,512]{2,0,1:T(8,128)(2,1)}, u32[]{:S(2)}, u32[]{:S(2)}) async-start(bf16[256,16,512]{2,0,1:T(8,128)(2,1)} %copy_select_fusion), calls=%async_computation.1 | async-start | bytes 8388608 | tf_op jit(solution)/shard_map/all_to_all | solution.py:39
  176.0 92.0 %all-to-all-done.1 = bf16[256,16,512]{2,0,1:T(8,128)(2,1)} async-done(((bf16[256,16,512]{2,0,1:T(8,128)(2,1)}), bf16[256,16,512]{2,0,1:T(8,128)(2,1)}, u32[]{:S(2)}, u32[]{:S(2)}) %all-to-all-start.1) | async-done | bytes 4194336 | tf_op jit(solution)/shard_map/all_to_all | solution.py:39
  268.0 6.4 %copy.63 = bf16[256,16,512]{0,2,1:T(8,128)(2,1)} copy(bf16[256,16,512]{2,0,1:T(8,128)(2,1)} %all-to-all-done.1) | data formatting | bytes 8388608 | tf_op jit(solution)/shard_map/all_to_all | solution.py:39
  274.4 4.4 %bitcast_select_fusion.1 = bf16[256,8192]{0,1:T(8,128)(2,1)} fusion(bf16[256,16,512]{0,2,1:T(8,128)(2,1)} %copy.63, pred[256]{0:T(512)(128)(4,1)S(1)} %broadcast_bitcast_fusion), kind=kLoop, calls=%fused_computation.8 | loop fusion | flops 2097152 | bytes 8388864 | tf_op jit(solution)/shard_map/jit(_where)/select_n | solution.py:80
  278.8 6.3 %copy.64 = bf16[256,8192]{1,0:T(8,128)(2,1)} copy(bf16[256,8192]{0,1:T(8,128)(2,1)} %bitcast_select_fusion.1) | data formatting | bytes 8388608 | tf_op jit(solution)/shard_map/jit(_where)/select_n | solution.py:80
  (35 shorter events, 1.0 us)
Async XLA Ops:
  0.0 24.9 %copy-start.4 = (s32[128]{0:T(128)S(1)}, s32[128]{0:T(128)}, u32[]{:S(2)}) copy-start(s32[128]{0:T(128)} %param.7) | copy-start | bytes 1540
  0.7 18.0 %collective-permute-start.4 = (s32[128]{0:T(128)S(1)}, s32[128]{0:T(128)S(1)}, u32[]{:S(2)}, u32[]{:S(2)}) collective-permute-start(s32[128]{0:T(128)S(1)} %broadcast_add_fusion), channel_id=1, source_target_pairs={{0,4},{1,5},{2,6},{3,7},{4,8},{5,9},{6,10},{7,11},{8,12},{9,13},{1... | collective-permute-start | bytes 1544 | tf_op jit(solution)/shard_map/ppermute | solution.py:16
  3.9 16.8 %collective-permute-start.5 = (s32[128]{0:T(128)S(1)}, s32[128]{0:T(128)S(1)}, u32[]{:S(2)}, u32[]{:S(2)}) collective-permute-start(s32[128]{0:T(128)S(1)} %broadcast_add_fusion), channel_id=1, source_target_pairs={{0,3},{1,4},{2,5},{3,6},{4,7},{5,8},{6,9},{7,10},{8,11},{9,12},{10... | collective-permute-start | bytes 1544 | tf_op jit(solution)/shard_map/ppermute | solution.py:16
  8.0 14.7 %collective-permute-start.6 = (s32[128]{0:T(128)S(1)}, s32[128]{0:T(128)S(1)}, u32[]{:S(2)}, u32[]{:S(2)}) collective-permute-start(s32[128]{0:T(128)S(1)} %broadcast_add_fusion), channel_id=1, source_target_pairs={{0,2},{1,3},{2,4},{3,5},{4,6},{5,7},{6,8},{7,9},{8,10},{9,11},{10,... | collective-permute-start | bytes 1544 | tf_op jit(solution)/shard_map/ppermute | solution.py:16
  9.9 15.0 %collective-permute-start.7 = (s32[128]{0:T(128)S(1)}, s32[128]{0:T(128)S(1)}, u32[]{:S(2)}, u32[]{:S(2)}) collective-permute-start(s32[128]{0:T(128)S(1)} %broadcast_add_fusion), channel_id=1, source_target_pairs={{0,1},{1,2},{2,3},{3,4},{4,5},{5,6},{6,7},{7,8},{8,9},{9,10},{10,1... | collective-permute-start | bytes 1544 | tf_op jit(solution)/shard_map/ppermute | solution.py:16
  14.6 15.8 %collective-permute-start = (bf16[128,2048]{0,1:T(8,128)(2,1)S(1)}, bf16[128,2048]{0,1:T(8,128)(2,1)S(1)}, u32[]{:S(2)}, u32[]{:S(2)}) collective-permute-start(bf16[128,2048]{0,1:T(8,128)(2,1)S(1)} %copy.52), channel_id=1, source_target_pairs={{0,4},{1,5},{2,6},{3,7},{4,8},{5,9},{6,10},{7,11},{8,12},{9,13},{1... | collective-permute-start | bytes 1572872 | tf_op jit(solution)/shard_map/ppermute | solution.py:16
  18.8 20.7 %collective-permute-start.1 = (bf16[128,2048]{0,1:T(8,128)(2,1)S(1)}, bf16[128,2048]{0,1:T(8,128)(2,1)S(1)}, u32[]{:S(2)}, u32[]{:S(2)}) collective-permute-start(bf16[128,2048]{0,1:T(8,128)(2,1)S(1)} %copy.52), channel_id=1, source_target_pairs={{0,3},{1,4},{2,5},{3,6},{4,7},{5,8},{6,9},{7,10},{8,11},{9,12},{10... | collective-permute-start | bytes 1572872 | tf_op jit(solution)/shard_map/ppermute | solution.py:16
  20.7 29.8 %collective-permute-start.2 = (bf16[128,2048]{0,1:T(8,128)(2,1)S(1)}, bf16[128,2048]{0,1:T(8,128)(2,1)S(1)}, u32[]{:S(2)}, u32[]{:S(2)}) collective-permute-start(bf16[128,2048]{0,1:T(8,128)(2,1)S(1)} %copy.52), channel_id=1, source_target_pairs={{0,2},{1,3},{2,4},{3,5},{4,6},{5,7},{6,8},{7,9},{8,10},{9,11},{10,... | collective-permute-start | bytes 1572872 | tf_op jit(solution)/shard_map/ppermute | solution.py:16
  22.7 33.4 %collective-permute-start.3 = (bf16[128,2048]{0,1:T(8,128)(2,1)S(1)}, bf16[128,2048]{0,1:T(8,128)(2,1)S(1)}, u32[]{:S(2)}, u32[]{:S(2)}) collective-permute-start(bf16[128,2048]{0,1:T(8,128)(2,1)S(1)} %copy.52), channel_id=1, source_target_pairs={{0,1},{1,2},{2,3},{3,4},{4,5},{5,6},{6,7},{7,8},{8,9},{9,10},{10,1... | collective-permute-start | bytes 1572872 | tf_op jit(solution)/shard_map/ppermute | solution.py:16
  25.1 38.7 %copy-start.2 = (pred[128,640]{0,1:T(8,128)(4,1)}, pred[128,640]{0,1:T(8,128)(4,1)S(1)}, u32[]{:S(2)}) copy-start(pred[128,640]{0,1:T(8,128)(4,1)S(1)} %fusion.11) | copy-start | bytes 245764
  56.3 1.5 copy-start.1
  77.2 6.8 %copy-start.3 = (s32[1,2]{1,0:T(1,128)S(1)}, s32[1,2]{1,0:T(1,128)}, u32[]{:S(2)}) copy-start(s32[1,2]{1,0:T(1,128)} %param.8) | copy-start | bytes 28
  77.2 64.1 %all-to-all-start = ((bf16[128,16,512]{0,2,1:T(8,128)(2,1)}), bf16[128,16,512]{0,2,1:T(8,128)(2,1)S(1)}, u32[]{:S(2)}, u32[]{:S(2)}) async-start(bf16[128,16,512]{0,2,1:T(8,128)(2,1)} %bitcast.74), calls=%async_computation | async-start | bytes 4194304 | tf_op jit(solution)/shard_map/all_to_all | solution.py:75
  141.4 1.3 copy-start
  170.4 97.6 %all-to-all-start.1 = ((bf16[256,16,512]{2,0,1:T(8,128)(2,1)}), bf16[256,16,512]{2,0,1:T(8,128)(2,1)}, u32[]{:S(2)}, u32[]{:S(2)}) async-start(bf16[256,16,512]{2,0,1:T(8,128)(2,1)} %copy_select_fusion), calls=%async_computation.1 | async-start | bytes 8388608 | tf_op jit(solution)/shard_map/all_to_all | solution.py:39
where the time goes:
time: 286 us; the launch traced here: 285 us
  waiting for transfers between devices  123 us (43%)
  blocking collectives  56.9 us (20%)
  local copies, waits for them, and re-layouts  40.1 us (14%)
  starting transfers between devices  32.2 us (11%)
  other arithmetic  18.6 us (7%)
  matrix products  13.7 us (5%)
    all_to_all x1, waiting for transfers between devices, deliver_owners(): lax.all_to_all(send_rows, 'seq', split_axis=1, concat_axis=1, tiled=True)  92 us
    all_gather x1, blocking collectives, local(): all_lists = lax.all_gather(owner_tiles, 'seq', axis=0, tiled=True)  56.9 us
    ppermute x8, waiting for transfers between devices, from_behind(): return lax.ppermute(shard, axis, pairs)  30.7 us
    ppermute x8, starting transfers between devices, from_behind(): return lax.ppermute(shard, axis, pairs)  20.5 us
    gather x1, local copies, waits for them, and re-layouts, deliver_owners(): jnp.take(head_rows, row_index.reshape(slot_rows, seq_count), axis=0)  17.3 us
    dot_general x1, matrix products, attend(): jnp.einsum('hgrk,khd->rhgd', weights, value_rows, preferred_element_type=...  7.78 us
    select_n x2, other arithmetic, deliver_owners(): jnp.take(head_rows, row_index.reshape(slot_rows, seq_count), axis=0)  7.62 us
    all_to_all x1, starting transfers between devices, local(): lax.all_to_all(out_send, 'seq', split_axis=1, concat_axis=0, tiled=True)  6.8 us
  transfers between devices with their start and end apart: 10, of which 5 were waited for; matrix products, arithmetic and copies ran while one was open for 2% of the time, Pallas kernels for 0%

commit v1 on v0

--- a/solution.py
+++ b/solution.py
@@ -31,12 +31,24 @@
 
 
 def deliver_owners(head_rows, all_lists, owner_tiles, seq_count, width):
+
+    def _produce_chunk(vals):
+        return jnp.concatenate(
+            jax.lax.all_to_all(
+                jnp.stack(jnp.split(vals, jax.lax.axis_size("seq"), 1), axis=0),
+                "seq",
+                split_axis=0,
+                concat_axis=0,
+            ),
+            1,
+        )
+
     slots_dev = owner_tiles.shape[1]
     slot_rows = slots_dev * TILE
     tile_rows = jnp.arange(TILE, dtype=jnp.int32)
     row_index = jnp.transpose(all_lists)[:, None, :] * TILE + tile_rows[None, :, None]
     send_rows = jnp.take(head_rows, row_index.reshape(slot_rows, seq_count), axis=0)
-    received = lax.all_to_all(send_rows, "seq", split_axis=1, concat_axis=1, tiled=True)
+    received = _produce_chunk(send_rows)
     return received.reshape(slot_rows, width)
 
 

time: 286 us -> 296 us (1.035)
  local copies, waits for them, and re-layouts: 40.1 us -> 51.6 us
    unnamed x20 -> x35, local copies, waits for them, and re-layouts: 6.79 us -> 17.6 us
    all_to_all x1 -> x0, local copies, waits for them, and re-layouts: 6.38 us -> none  [deliver_owners(): lax.all_to_all(send_rows, 'seq', split_axis=1, concat_axis=1, tiled=True)]
    reshape x0 -> x1, local copies, waits for them, and re-layouts: none -> 6.38 us  [_produce_chunk(): jnp.concatenate(jax.lax.all_to_all(jnp.stack(jnp.split(vals, jax.lax.axis...]
where the time goes in v1:
time: 296 us; the launch traced here: 295 us
  waiting for transfers between devices  123 us (42%)
  blocking collectives  56.9 us (19%)
  local copies, waits for them, and re-layouts  51.6 us (17%)
  starting transfers between devices  32.2 us (11%)
  other arithmetic  17.3 us (6%)
  matrix products  13.7 us (5%)
    all_to_all x1, waiting for transfers between devices, _produce_chunk(): jax.lax.all_to_all(jnp.stack(jnp.split(vals, jax.lax.axis_size('seq'), 1)...  92 us
    all_gather x1, blocking collectives, local(): all_lists = lax.all_gather(owner_tiles, 'seq', axis=0, tiled=True)  56.9 us
    ppermute x8, waiting for transfers between devices, from_behind(): return lax.ppermute(shard, axis, pairs)  30.7 us
    ppermute x8, starting transfers between devices, from_behind(): return lax.ppermute(shard, axis, pairs)  20.5 us
    unnamed x35, local copies, waits for them, and re-layouts  17.6 us
    gather x1, local copies, waits for them, and re-layouts, deliver_owners(): jnp.take(head_rows, row_index.reshape(slot_rows, seq_count), axis=0)  17.3 us
    dot_general x1, matrix products, attend(): jnp.einsum('hgrk,khd->rhgd', weights, value_rows, preferred_element_type=...  7.78 us
    all_to_all x1, starting transfers between devices, local(): lax.all_to_all(out_send, 'seq', split_axis=1, concat_axis=0, tiled=True)  6.8 us
  transfers between devices with their start and end apart: 10, of which 5 were waited for; matrix products, arithmetic and copies ran while one was open for 2% of the time, Pallas kernels for 0%

profile of v1, /device:TPU:15, one launch (start us, length us, event | category | flops | bytes accessed | tf_op | source)
XLA Modules:
  0.0 295.4 jit_solution(4063693266577255053)
XLA Ops:
  0.0 0.7 broadcast_add_fusion
  0.7 3.2 %collective-permute-start.4 = (s32[128]{0:T(128)S(1)}, s32[128]{0:T(128)S(1)}, u32[]{:S(2)}, u32[]{:S(2)}) collective-permute-start(s32[128]{0:T(128)S(1)} %broadcast_add_fusion), channel_id=1, source_target_pairs={{0,4},{1,5},{2,6},{3,7},{4,8},{5,9},{6,10},{7,11},{8,12},{9,13},{1... | collective-permute-start | bytes 1544 | tf_op jit(solution)/shard_map/ppermute | solution.py:16
  3.9 4.0 %collective-permute-start.5 = (s32[128]{0:T(128)S(1)}, s32[128]{0:T(128)S(1)}, u32[]{:S(2)}, u32[]{:S(2)}) collective-permute-start(s32[128]{0:T(128)S(1)} %broadcast_add_fusion), channel_id=1, source_target_pairs={{0,3},{1,4},{2,5},{3,6},{4,7},{5,8},{6,9},{7,10},{8,11},{9,12},{10... | collective-permute-start | bytes 1544 | tf_op jit(solution)/shard_map/ppermute | solution.py:16
  8.0 1.9 collective-permute-start.6
  9.9 3.4 %collective-permute-start.7 = (s32[128]{0:T(128)S(1)}, s32[128]{0:T(128)S(1)}, u32[]{:S(2)}, u32[]{:S(2)}) collective-permute-start(s32[128]{0:T(128)S(1)} %broadcast_add_fusion), channel_id=1, source_target_pairs={{0,1},{1,2},{2,3},{3,4},{4,5},{5,6},{6,7},{7,8},{8,9},{9,10},{10,1... | collective-permute-start | bytes 1544 | tf_op jit(solution)/shard_map/ppermute | solution.py:16
  13.3 1.3 copy.72
  14.6 1.9 collective-permute-start
  16.6 2.2 copy.91
  18.8 1.9 collective-permute-start.1
  20.7 1.9 collective-permute-start.2
  22.7 2.2 collective-permute-start.3
  25.1 5.3 %collective-permute-done = bf16[128,2048]{0,1:T(8,128)(2,1)S(1)} collective-permute-done((bf16[128,2048]{0,1:T(8,128)(2,1)S(1)}, bf16[128,2048]{0,1:T(8,128)(2,1)S(1)}, u32[]{:S(2)}, u32[]{:S(2)}) %collective-permute-start) | collective-permute-done | bytes 524320 | tf_op jit(solution)/shard_map/ppermute | solution.py:16
  30.5 9.0 %collective-permute-done.1 = bf16[128,2048]{0,1:T(8,128)(2,1)S(1)} collective-permute-done((bf16[128,2048]{0,1:T(8,128)(2,1)S(1)}, bf16[128,2048]{0,1:T(8,128)(2,1)S(1)}, u32[]{:S(2)}, u32[]{:S(2)}) %collective-permute-start.1) | collective-permute-done | bytes 524320 | tf_op jit(solution)/shard_map/ppermute | solution.py:16
  39.6 10.8 %collective-permute-done.2 = bf16[128,2048]{0,1:T(8,128)(2,1)S(1)} collective-permute-done((bf16[128,2048]{0,1:T(8,128)(2,1)S(1)}, bf16[128,2048]{0,1:T(8,128)(2,1)S(1)}, u32[]{:S(2)}, u32[]{:S(2)}) %collective-permute-start.2) | collective-permute-done | bytes 524320 | tf_op jit(solution)/shard_map/ppermute | solution.py:16
  50.6 5.5 %collective-permute-done.3 = bf16[128,2048]{0,1:T(8,128)(2,1)S(1)} collective-permute-done((bf16[128,2048]{0,1:T(8,128)(2,1)S(1)}, bf16[128,2048]{0,1:T(8,128)(2,1)S(1)}, u32[]{:S(2)}, u32[]{:S(2)}) %collective-permute-start.3) | collective-permute-done | bytes 524320 | tf_op jit(solution)/shard_map/ppermute | solution.py:16
  56.4 1.5 copy-done.1
  57.8 5.9 %fusion.2 = (f32[8,8,128]{2,1,0:T(8,128)S(1)}, f32[8,640,128,8]{2,1,3,0:T(8,128)S(1)}) fusion(pred[128,640]{0,1:T(8,128)(4,1)S(1)} %fusion.11, bf16[128,8,8,128]{3,2,1,0:T(8,128)(2,1)S(1)} %bitcast.134, bf16[640,8,2,128]{0,3,2,1:T(8,128)(2,1)} %bitcast.136), kind=kOutput, calls=%fused_computation.5 | convolution fusion | flops 1357897728 | bytes 24494080 | tf_op jit(solution)/shard_map/rhgd,khd->hgrk/dot_general | solution.py:21
  63.8 5.7 %fusion = f32[8,8,128]{2,1,0:T(8,128)} fusion(f32[8,640,128,8]{2,1,3,0:T(8,128)S(1)} %get-tuple-element.6, f32[8,8,128]{2,1,0:T(8,128)S(1)} %get-tuple-element.5, pred[128,640]{0,1:T(8,128)(4,1)S(1)} %fusion.11), kind=kLoop, calls=%fused_computation.3 | loop fusion | flops 20963328 | bytes 21118976 | tf_op jit(solution)/shard_map/reduce_sum | solution.py:25
  69.5 7.8 %fusion.6 = bf16[128,8,8,128]{0,3,2,1:T(8,128)(2,1)} fusion(f32[8,640,128,8]{2,1,3,0:T(8,128)S(1)} %get-tuple-element.6, f32[8,8,128]{2,1,0:T(8,128)S(1)} %get-tuple-element.5, pred[128,640]{0,1:T(8,128)(4,1)} %copy-done.2, f32[128,8,8]{0,2,1:T(8,128)} %bitcast.141, bf16[640,8,2,128]{0,3,2,1:T(8,128)(2,1)} %bitcast.137), kind=kOutput, calls=%fused_computation.10 | convolution fusion | flops 1365245952 | bytes 24526848 | tf_op jit(solution)/shard_map/hgrk,khd->rhgd/dot_general | solution.py:27
  77.2 6.8 %all-to-all-start = ((bf16[128,16,512]{0,2,1:T(8,128)(2,1)}), bf16[128,16,512]{0,2,1:T(8,128)(2,1)S(1)}, u32[]{:S(2)}, u32[]{:S(2)}) async-start(bf16[128,16,512]{0,2,1:T(8,128)(2,1)} %bitcast.139), calls=%async_computation | async-start | bytes 4194304 | tf_op jit(solution)/shard_map/all_to_all | solution.py:87
  84.1 56.9 %all-gather = s32[16,1,2]{2,1,0:T(1,128)S(1)} all-gather(s32[1,1,2]{2,1,0:T(1,128)S(1)} %bitcast.142), channel_id=1, replica_groups=mesh['groups'=2,'seq'=16] {'seq'}, dimensions={0}, use_global_device_ids=true | all-gather | bytes 136 | tf_op jit(solution)/shard_map/all_gather | solution.py:85
  141.4 1.3 copy-done
  142.7 2.9 copy.81
  145.5 17.3 %gather_fusion = bf16[4096,512]{1,0:T(8,128)(2,1)} fusion(bf16[2048,512]{1,0:T(8,128)(2,1)S(1)} %bitcast.132, s32[4096]{0:T(1024)S(1)} %broadcast_clamp_fusion), kind=kCustom, calls=%fused_computation | custom fusion | bytes 8404992 | tf_op jit(solution)/shard_map/jit(_take)/gather | solution.py:50
  162.9 6.2 %copy_select_fusion = bf16[256,16,512]{2,0,1:T(8,128)(2,1)S(1)} fusion(bf16[256,16,512]{2,1,0:T(8,128)(2,1)} %bitcast.133, pred[256,16]{0,1:T(8,128)(4,1)S(1)} %compare_and_fusion), kind=kLoop, calls=%fused_computation.11 | loop fusion | flops 2097152 | bytes 8392704 | tf_op jit(solution)/shard_map/jit(_take)/select_n | solution.py:50
  169.1 0.7 fusion.27
  169.8 0.7 fusion.26
  180.6 4.9 %all-to-all-start.1 = ((bf16[16,256,1,512]{3,1,2,0:T(8,128)(2,1)}), bf16[16,256,1,512]{3,1,2,0:T(8,128)(2,1)}, u32[]{:S(2)}, u32[]{:S(2)}) async-start(bf16[16,256,1,512]{3,1,2,0:T(8,128)(2,1)} %fusion.12), calls=%async_computation.1 | async-start | bytes 8388608 | tf_op jit(solution)/shard_map/all_to_all | solution.py:37
  186.2 92.0 %all-to-all-done.1 = bf16[16,256,1,512]{3,1,2,0:T(8,128)(2,1)} async-done(((bf16[16,256,1,512]{3,1,2,0:T(8,128)(2,1)}), bf16[16,256,1,512]{3,1,2,0:T(8,128)(2,1)}, u32[]{:S(2)}, u32[]{:S(2)}) %all-to-all-start.1) | async-done | bytes 4194336 | tf_op jit(solution)/shard_map/all_to_all | solution.py:37
  278.2 6.4 %copy.83 = bf16[256,16,1,512]{0,3,1,2:T(8,128)(2,1)} copy(bf16[256,16,1,512]{3,0,2,1:T(8,128)(2,1)} %bitcast.41) | data formatting | bytes 8388608 | tf_op jit(solution)/shard_map/reshape | solution.py:36
  284.6 4.4 %bitcast_select_fusion.1 = bf16[256,8192]{0,1:T(8,128)(2,1)} fusion(bf16[256,16,1,512]{0,3,1,2:T(8,128)(2,1)} %copy.83, pred[256]{0:T(512)(128)(4,1)S(1)} %broadcast_bitcast_fusion), kind=kLoop, calls=%fused_computation.8 | loop fusion | flops 2097152 | bytes 8388864 | tf_op jit(solution)/shard_map/jit(_where)/select_n | solution.py:92
  289.0 6.3 %copy.84 = bf16[256,8192]{1,0:T(8,128)(2,1)} copy(bf16[256,8192]{0,1:T(8,128)(2,1)} %bitcast_select_fusion.1) | data formatting | bytes 8388608 | tf_op jit(solution)/shard_map/jit(_where)/select_n | solution.py:92
  (51 shorter events, 11.3 us)
Async XLA Ops:
  0.0 24.9 %copy-start.4 = (s32[128]{0:T(128)S(1)}, s32[128]{0:T(128)}, u32[]{:S(2)}) copy-start(s32[128]{0:T(128)} %param.7) | copy-start | bytes 1540
  0.7 18.0 %collective-permute-start.4 = (s32[128]{0:T(128)S(1)}, s32[128]{0:T(128)S(1)}, u32[]{:S(2)}, u32[]{:S(2)}) collective-permute-start(s32[128]{0:T(128)S(1)} %broadcast_add_fusion), channel_id=1, source_target_pairs={{0,4},{1,5},{2,6},{3,7},{4,8},{5,9},{6,10},{7,11},{8,12},{9,13},{1... | collective-permute-start | bytes 1544 | tf_op jit(solution)/shard_map/ppermute | solution.py:16
  3.9 16.8 %collective-permute-start.5 = (s32[128]{0:T(128)S(1)}, s32[128]{0:T(128)S(1)}, u32[]{:S(2)}, u32[]{:S(2)}) collective-permute-start(s32[128]{0:T(128)S(1)} %broadcast_add_fusion), channel_id=1, source_target_pairs={{0,3},{1,4},{2,5},{3,6},{4,7},{5,8},{6,9},{7,10},{8,11},{9,12},{10... | collective-permute-start | bytes 1544 | tf_op jit(solution)/shard_map/ppermute | solution.py:16
  8.0 14.7 %collective-permute-start.6 = (s32[128]{0:T(128)S(1)}, s32[128]{0:T(128)S(1)}, u32[]{:S(2)}, u32[]{:S(2)}) collective-permute-start(s32[128]{0:T(128)S(1)} %broadcast_add_fusion), channel_id=1, source_target_pairs={{0,2},{1,3},{2,4},{3,5},{4,6},{5,7},{6,8},{7,9},{8,10},{9,11},{10,... | collective-permute-start | bytes 1544 | tf_op jit(solution)/shard_map/ppermute | solution.py:16
  9.9 15.0 %collective-permute-start.7 = (s32[128]{0:T(128)S(1)}, s32[128]{0:T(128)S(1)}, u32[]{:S(2)}, u32[]{:S(2)}) collective-permute-start(s32[128]{0:T(128)S(1)} %broadcast_add_fusion), channel_id=1, source_target_pairs={{0,1},{1,2},{2,3},{3,4},{4,5},{5,6},{6,7},{7,8},{8,9},{9,10},{10,1... | collective-permute-start | bytes 1544 | tf_op jit(solution)/shard_map/ppermute | solution.py:16
  14.6 15.8 %collective-permute-start = (bf16[128,2048]{0,1:T(8,128)(2,1)S(1)}, bf16[128,2048]{0,1:T(8,128)(2,1)S(1)}, u32[]{:S(2)}, u32[]{:S(2)}) collective-permute-start(bf16[128,2048]{0,1:T(8,128)(2,1)S(1)} %copy.72), channel_id=1, source_target_pairs={{0,4},{1,5},{2,6},{3,7},{4,8},{5,9},{6,10},{7,11},{8,12},{9,13},{1... | collective-permute-start | bytes 1572872 | tf_op jit(solution)/shard_map/ppermute | solution.py:16
  18.8 20.7 %collective-permute-start.1 = (bf16[128,2048]{0,1:T(8,128)(2,1)S(1)}, bf16[128,2048]{0,1:T(8,128)(2,1)S(1)}, u32[]{:S(2)}, u32[]{:S(2)}) collective-permute-start(bf16[128,2048]{0,1:T(8,128)(2,1)S(1)} %copy.72), channel_id=1, source_target_pairs={{0,3},{1,4},{2,5},{3,6},{4,7},{5,8},{6,9},{7,10},{8,11},{9,12},{10... | collective-permute-start | bytes 1572872 | tf_op jit(solution)/shard_map/ppermute | solution.py:16
  20.7 29.8 %collective-permute-start.2 = (bf16[128,2048]{0,1:T(8,128)(2,1)S(1)}, bf16[128,2048]{0,1:T(8,128)(2,1)S(1)}, u32[]{:S(2)}, u32[]{:S(2)}) collective-permute-start(bf16[128,2048]{0,1:T(8,128)(2,1)S(1)} %copy.72), channel_id=1, source_target_pairs={{0,2},{1,3},{2,4},{3,5},{4,6},{5,7},{6,8},{7,9},{8,10},{9,11},{10,... | collective-permute-start | bytes 1572872 | tf_op jit(solution)/shard_map/ppermute | solution.py:16
  22.7 33.4 %collective-permute-start.3 = (bf16[128,2048]{0,1:T(8,128)(2,1)S(1)}, bf16[128,2048]{0,1:T(8,128)(2,1)S(1)}, u32[]{:S(2)}, u32[]{:S(2)}) collective-permute-start(bf16[128,2048]{0,1:T(8,128)(2,1)S(1)} %copy.72), channel_id=1, source_target_pairs={{0,1},{1,2},{2,3},{3,4},{4,5},{5,6},{6,7},{7,8},{8,9},{9,10},{10,1... | collective-permute-start | bytes 1572872 | tf_op jit(solution)/shard_map/ppermute | solution.py:16
  25.1 38.7 %copy-start.2 = (pred[128,640]{0,1:T(8,128)(4,1)}, pred[128,640]{0,1:T(8,128)(4,1)S(1)}, u32[]{:S(2)}) copy-start(pred[128,640]{0,1:T(8,128)(4,1)S(1)} %fusion.11) | copy-start | bytes 245764
  56.3 1.5 copy-start.1
  77.2 6.8 %copy-start.3 = (s32[1,2]{1,0:T(1,128)S(1)}, s32[1,2]{1,0:T(1,128)}, u32[]{:S(2)}) copy-start(s32[1,2]{1,0:T(1,128)} %param.8) | copy-start | bytes 28
  77.2 64.1 %all-to-all-start = ((bf16[128,16,512]{0,2,1:T(8,128)(2,1)}), bf16[128,16,512]{0,2,1:T(8,128)(2,1)S(1)}, u32[]{:S(2)}, u32[]{:S(2)}) async-start(bf16[128,16,512]{0,2,1:T(8,128)(2,1)} %bitcast.139), calls=%async_computation | async-start | bytes 4194304 | tf_op jit(solution)/shard_map/all_to_all | solution.py:87
  141.4 1.3 copy-start
  180.6 97.6 %all-to-all-start.1 = ((bf16[16,256,1,512]{3,1,2,0:T(8,128)(2,1)}), bf16[16,256,1,512]{3,1,2,0:T(8,128)(2,1)}, u32[]{:S(2)}, u32[]{:S(2)}) async-start(bf16[16,256,1,512]{3,1,2,0:T(8,128)(2,1)} %fusion.12), calls=%async_computation.1 | async-start | bytes 8388608 | tf_op jit(solution)/shard_map/all_to_all | solution.py:37
